TPU v7x, 256 devices: a whole 4x4x8 slice. The times are simulated.
256 devices in a mesh: grp: 4 (over z_hi, core), pen: 64 (over z_lo, x, y).
Axes of the slice: x: 4, y: 4, z: 8 (z_hi: 2, z_lo: 4; z = z_hi * 4 + z_lo), core: 2. Of those that a mesh axis runs over, the one named last changes fastest.
Arguments:
- u_field: float32 [2, 2048, 2048], P(None, ('grp', 'pen')), may hold values from -6 to 6
- v_field: float32 [2, 2048, 2048], P(None, ('grp', 'pen')), may hold values from -6 to 6
- ky_order: int32 [2048], replicated, may hold values from 0 to 2047, as said below
Outputs:
- deriv: float32 [2048, 2, 2, 2048], P('grp', None, None, 'pen')
Inputs may be any that keep to these rules, and one draw needn't show every extreme that they name: ky_order is a permutation of 0 to 2047; for every position j, ky_order[2047 - j] = (2048 - ky_order[j]) mod 2048, except for the one pair of positions that holds 0 and 1024.
All inputs are finite; a program needn't handle non-finite values.
Results may differ from a plain program's by a relative error of at most 0.00007.
Values sent between devices are 32-bit elements; how exact they have to be, the bound alone decides.
A program may use at most 64 MiB of HBM per device.

v0:
```python
import math

import jax
import jax.numpy as jnp
from jax import lax
from jax.sharding import PartitionSpec as P

two_pi = 2.0 * math.pi


def partner_2(block, axis, bit):
    count = lax.axis_size(axis)
    route = []
    for low in range(count):
        high = low | 1 << bit
        if high != low and high < count:
            route += [(low, high), (high, low)]
    return lax.ppermute(block, axis, route)


def signed_scale(waves, length):
    signed = jnp.where(waves < length // 2, waves, waves - length)
    signed = jnp.where(waves == length // 2, 0, signed)
    return 2.0 / length * signed.astype(jnp.float32)


def twiddle(row_values, column_values, length):
    residue = row_values[:, None] * column_values[None, :] % length
    angles = two_pi / length * residue.astype(jnp.float32)
    return (jnp.cos(angles), jnp.sin(angles))


def wave_numbers(position, length):
    half_length = length // 2
    upper_side = position >= half_length
    pair_index = jnp.where(upper_side, length - 1 - position, position)
    upper_value = jnp.where(pair_index > 0, length - pair_index, half_length)
    return (jnp.where(upper_side, upper_value, pair_index), pair_index == 0)


def on_device(u_field, v_field, ky_order):
    planes, entry_rows, length_y = u_field.shape
    pen_size = lax.axis_size("pen")
    group_size = lax.axis_size("grp")
    quarter = lax.axis_index("grp")
    slab_rows = length_y // pen_size
    group_rows = entry_rows * pen_size
    length_z = group_rows * group_size
    column_count = planes * slab_rows
    exact_mode = lax.Precision.HIGHEST
    stacked = jnp.concatenate([u_field, v_field], 0).reshape(2 * planes * entry_rows, length_y)
    positions_y = lax.iota(jnp.int32, length_y)
    block_width = min(length_y, 128)
    block_count = length_y // block_width

    def row_block(first_row):
        waves_y = lax.dynamic_slice_in_dim(ky_order, first_row, block_width)
        cosines, sines = twiddle(positions_y, waves_y, length_y)
        tables = jnp.concatenate([cosines, sines], 1)
        return jnp.dot(stacked, tables, precision=exact_mode, preferred_element_type=jnp.float32)

    blocks = lax.map(row_block, jnp.arange(block_count, dtype=jnp.int32) * block_width)
    pieces = blocks.reshape(block_count, 2, planes * entry_rows, 2, block_width)
    norm_y = 1.0 / math.sqrt(length_y)

    def to_layout(values):
        return (norm_y * jnp.transpose(values, (1, 0, 2))).reshape(planes, entry_rows, length_y)

    real_rows = to_layout(pieces[:, 0, :, 0] + pieces[:, 1, :, 1])
    imaginary_rows = to_layout(pieces[:, 1, :, 0] - pieces[:, 0, :, 1])

    def as_columns(values):
        return jnp.transpose(values, (1, 0, 2)).reshape(group_rows, column_count)

    my_waves_y = lax.dynamic_slice_in_dim(ky_order, lax.axis_index("pen") * slab_rows, slab_rows)
    self_y = (my_waves_y == 0) | (my_waves_y == length_y // 2)
    own_z = quarter * group_rows + lax.iota(jnp.int32, group_rows)
    own_waves_z, self_z = wave_numbers(own_z, length_z)
    norm_z = 1.0 / math.sqrt(length_z)
    received = (
        lax.all_to_all(real_rows, "pen", split_axis=2, concat_axis=1, tiled=True),
        lax.all_to_all(imaginary_rows, "pen", split_axis=2, concat_axis=1, tiled=True),
    )
    right_side = jnp.concatenate([as_columns(values) for values in received], 1)
    pair_count = len(received) // 2
    block_rows = math.gcd(group_rows * lax.axis_size("grp"), 256)

    def forward_block_term(offset):
        position = offset + lax.iota(jnp.int32, block_rows)
        waves_z, unused = wave_numbers(position, length_z)
        cosines, sines = twiddle(waves_z, own_z, length_z)
        left_side = jnp.concatenate([cosines, sines], 0)
        product = jnp.dot(
            left_side, right_side, precision=exact_mode, preferred_element_type=jnp.float32
        )
        product = product.reshape(2, block_rows, pair_count, 2, column_count)
        real_part = product[0, :, :, 0] + product[1, :, :, 1]
        imaginary_part = product[0, :, :, 1] - product[1, :, :, 0]
        return norm_z * jnp.stack([real_part, imaginary_part], 2).reshape(block_rows, -1)

    offsets = (
        jnp.arange(group_rows * lax.axis_size("grp") // block_rows, dtype=jnp.int32) * block_rows
    )
    spectrum = lax.psum_scatter(
        lax.map(forward_block_term, offsets).reshape(group_rows * lax.axis_size("grp"), -1),
        "grp",
        scatter_dimension=0,
        tiled=True,
    )
    own_part = spectrum.reshape(group_rows, 2, planes, slab_rows)
    partner = spectrum
    for level in range(pen_size.bit_length() - 1):
        partner = partner_2(partner, "pen", level)
    partner = jnp.flip(partner.reshape(group_rows, 2, planes, slab_rows), 3)
    chosen = jnp.where(self_y[None, None, None, :], own_part, partner)
    across = chosen.reshape(group_rows, -1)
    for level in range(group_size.bit_length() - 1):
        across = partner_2(across, "grp", level)
    across = across.reshape(chosen.shape)
    across = jnp.flip(across, 0)
    mirror = jnp.where(self_z[:, None, None, None], chosen, across)
    own_real, own_imag = (own_part[:, 0], own_part[:, 1])
    mirror_real, mirror_imag = (mirror[:, 0], mirror[:, 1])
    first_real = 0.5 * (own_real + mirror_real)
    first_imag = 0.5 * (own_imag - mirror_imag)
    second_real = 0.5 * (own_imag + mirror_imag)
    second_imag = -0.5 * (own_real - mirror_real)
    scale_y = signed_scale(my_waves_y, length_y)[None, None, :]
    scale_z = signed_scale(own_waves_z, length_z)[:, None, None]
    packed_real = -scale_y * first_imag - scale_z * second_real
    packed_imag = scale_y * first_real - scale_z * second_imag
    back_side = jnp.concatenate(
        [
            packed_real.reshape(group_rows, column_count),
            packed_imag.reshape(group_rows, column_count),
        ],
        1,
    )
    inverse_block_rows = math.gcd(group_rows * lax.axis_size("grp"), 256)

    def inverse_block_term(offset):
        position = offset + lax.iota(jnp.int32, inverse_block_rows)
        cosines, sines = twiddle(position, own_waves_z, length_z)
        left_side = jnp.concatenate([cosines, sines], 0)
        product = jnp.dot(
            left_side, back_side, precision=exact_mode, preferred_element_type=jnp.float32
        )
        product = product.reshape(2, inverse_block_rows, 2, column_count)
        real_part = product[0, :, 0] - product[1, :, 1]
        imaginary_part = product[0, :, 1] + product[1, :, 0]
        return norm_z * jnp.stack([real_part, imaginary_part], 1).reshape(inverse_block_rows, -1)

    offsets = (
        jnp.arange(group_rows * lax.axis_size("grp") // inverse_block_rows, dtype=jnp.int32)
        * inverse_block_rows
    )
    result = lax.psum_scatter(
        lax.map(inverse_block_term, offsets).reshape(group_rows * lax.axis_size("grp"), -1),
        "grp",
        scatter_dimension=0,
        tiled=True,
    )
    return result.reshape(group_rows, 2, planes, slab_rows)


def solution(mesh):
    placed = (P(None, ("grp", "pen"), None), P(None, ("grp", "pen"), None), P())
    return jax.shard_map(
        on_device,
        mesh=mesh,
        in_specs=placed,
        out_specs=P("grp", None, None, "pen"),
        check_vma=False,
    )
```

profile of v0, /device:TPU:1, one launch (start us, length us, event | category | flops | bytes accessed | tf_op | source)
XLA Modules:
  0.0 485.3 jit_solution(10980997881373566586)
XLA Ops:
  7.5 141.3 %while.39 = (s32[]{:T(128)}, f32[16,32,256]{2,1,0:T(8,128)S(1)}, s32[16]{0:T(128)S(1)}, s32[2048]{0:T(1024)}, f32[32,2048]{1,0:T(8,128)S(1)}, /*index=5*/s32[]{:T(128)}, s32[]{:T(128)}, s32[]{:T(128)}) while((s32[]{:T(128)}, f32[16,32,256]{2,1,0:T(8,128)S(1)}, s32[16]{0:T(128)S(1)}, s32[2048]{0:T(1024)}, f32[32,2048]{1,0:T(8,128)S(1)}, ...), condition=%wide.region_1.2_spmd.clone, body=%wide.region_0.1_spmd.clone.sunk | while | flops 205520896 | bytes 4490891 | solution.py:62
  11.1 4.1 fusion.86
  19.9 4.1 fusion.86
  28.7 4.1 fusion.86
  37.6 4.1 fusion.86
  46.4 4.1 fusion.86
  55.2 4.1 fusion.86
  64.1 4.1 fusion.86
  72.9 4.1 fusion.86
  81.8 4.1 fusion.86
  90.6 4.1 fusion.86
  99.4 4.1 fusion.86
  108.2 4.1 fusion.86
  117.1 4.1 fusion.86
  125.9 4.1 fusion.86
  134.7 4.1 fusion.86
  143.6 4.1 fusion.86
  150.8 4.0 reshape.271
  154.8 12.7 %all-to-all-start.1 = ((f32[64,1,512]{2,1,0:T(1,128)}), f32[64,1,512]{2,1,0:T(1,128)S(1)}, u32[]{:S(2)}, u32[]{:S(2)}) async-start(f32[64,1,512]{2,1,0:T(1,128)} %reshape.271), calls=%async_computation.1 | async-start | bytes 262144 | tf_op jit(solution)/shard_map/all_to_all | solution.py:82
  168.6 4.0 reshape.273
  172.6 4.4 all-to-all-done.1
  177.0 5.6 %all-to-all-start = ((f32[64,1,512]{2,1,0:T(1,128)}), f32[64,1,512]{2,1,0:T(1,128)S(1)}, u32[]{:S(2)}, u32[]{:S(2)}) async-start(f32[64,1,512]{2,1,0:T(1,128)} %reshape.273), calls=%async_computation | async-start | bytes 262144 | tf_op jit(solution)/shard_map/all_to_all | solution.py:81
  184.2 3.2 reshape.272
  189.4 2.9 all-to-all-done
  193.2 3.2 reshape.274
  198.5 75.1 %while.40 = (s32[]{:T(128)}, f32[8,256,128]{1,0,2:T(8,128)}, s32[8]{0:T(128)S(1)}, f32[512,128]{1,0:T(8,128)S(1)}, s32[]{:T(128)}, /*index=5*/s32[]{:T(128)}, s32[]{:T(128)}) while((s32[]{:T(128)}, f32[8,256,128]{1,0,2:T(8,128)}, s32[8]{0:T(128)S(1)}, f32[512,128]{1,0:T(8,128)S(1)}, s32[]{:T(128)}, /*index=5*/s32[]{:T(128)}, ...), condition=%wide.region_3.4_spmd.clone, body=%wide.region_2.3_spmd.clone.sunk | while | flops 404851200 | bytes 4593765 | solution.py:105
  203.9 4.0 dynamic_update_slice.29
  213.3 4.0 dynamic_update_slice.29
  222.7 4.0 dynamic_update_slice.29
  232.1 4.0 dynamic_update_slice.29
  241.4 4.0 dynamic_update_slice.29
  250.8 4.0 dynamic_update_slice.29
  260.2 4.0 dynamic_update_slice.29
  269.6 4.0 dynamic_update_slice.29
  273.6 2.5 copy.108
  276.2 43.8 %reduce-scatter.3.cloned.1.call-done = f32[512,128]{0,1:T(8,128)} async-done(((f32[2048,128]{0,1:T(8,128)}), f32[512,128]{0,1:T(8,128)}) %reduce-scatter.3.cloned.1.call-update) | async-done | bytes 262160 | tf_op jit(solution)/shard_map/reduce_scatter | solution.py:104
  321.2 6.2 %collective-permute-done = f32[512,128]{0,1:T(8,128)S(1)} collective-permute-done((f32[512,128]{0,1:T(8,128)}, f32[512,128]{0,1:T(8,128)S(1)}, u32[]{:S(2)}, u32[]{:S(2)}) %collective-permute-start) | collective-permute-done | bytes 262176 | tf_op jit(solution)/shard_map/ppermute | solution.py:18
  327.4 2.7 collective-permute-start.1
  330.1 5.0 %collective-permute-done.1 = f32[512,128]{0,1:T(8,128)S(1)} collective-permute-done((f32[512,128]{0,1:T(8,128)S(1)}, f32[512,128]{0,1:T(8,128)S(1)}, u32[]{:S(2)}, u32[]{:S(2)}) %collective-permute-start.1) | collective-permute-done | bytes 262176 | tf_op jit(solution)/shard_map/ppermute | solution.py:18
  336.2 4.1 collective-permute-done.2
  340.3 2.6 collective-permute-start.3
  343.0 5.2 %collective-permute-done.3 = f32[512,128]{0,1:T(8,128)S(1)} collective-permute-done((f32[512,128]{0,1:T(8,128)S(1)}, f32[512,128]{0,1:T(8,128)S(1)}, u32[]{:S(2)}, u32[]{:S(2)}) %collective-permute-start.3) | collective-permute-done | bytes 262176 | tf_op jit(solution)/shard_map/ppermute | solution.py:18
  348.9 4.5 collective-permute-done.4
  354.4 8.0 %collective-permute-done.5 = f32[512,128]{0,1:T(8,128)S(1)} collective-permute-done((f32[512,128]{0,1:T(8,128)S(1)}, f32[512,128]{0,1:T(8,128)S(1)}, u32[]{:S(2)}, u32[]{:S(2)}) %collective-permute-start.5) | collective-permute-done | bytes 262176 | tf_op jit(solution)/shard_map/ppermute | solution.py:18
  363.5 6.7 %collective-permute-start.6 = (f32[512,128]{0,1:T(8,128)S(1)}, f32[512,128]{0,1:T(8,128)S(1)}, u32[]{:S(2)}, u32[]{:S(2)}) collective-permute-start(f32[512,128]{0,1:T(8,128)S(1)} %bitcast.149), channel_id=1, source_target_pairs={{0,64},{64,0},{128,192},{192,128},{1,65},{65,1},{129,193},{193,129... | collective-permute-start | bytes 786440 | tf_op jit(solution)/shard_map/ppermute | solution.py:18
  371.8 15.3 %collective-permute-done.7 = f32[512,128]{0,1:T(8,128)S(1)} collective-permute-done((f32[512,128]{0,1:T(8,128)S(1)}, f32[512,128]{0,1:T(8,128)S(1)}, u32[]{:S(2)}, u32[]{:S(2)}) %collective-permute-start.7) | collective-permute-done | bytes 262176 | tf_op jit(solution)/shard_map/ppermute | solution.py:18
  387.9 42.4 %while.41 = (s32[]{:T(128)}, f32[8,256,128]{2,1,0:T(8,128)S(1)}, s32[8]{0:T(128)S(1)}, f32[512,128]{1,0:T(8,128)S(1)}, s32[]{:T(128)}, /*index=5*/s32[]{:T(128)}) while((s32[]{:T(128)}, f32[8,256,128]{2,1,0:T(8,128)S(1)}, s32[8]{0:T(128)S(1)}, f32[512,128]{1,0:T(8,128)S(1)}, s32[]{:T(128)}, /*index=5*/s32[]{:T(128)}) %tuple.116), condition=%wide.region_6.7_spmd.clone, body=%wide.region_5.6_spmd.clone.sunk | while | flops 404852992 | bytes 4593757 | solution.py:158
  431.3 45.4 %reduce-scatter.5.cloned.1.call-done = f32[512,128]{1,0:T(8,128)} async-done(((f32[2048,128]{1,0:T(8,128)}), f32[512,128]{1,0:T(8,128)}) %reduce-scatter.5.cloned.1.call-update) | async-done | bytes 262160 | tf_op jit(solution)/shard_map/reduce_scatter | solution.py:157
  (287 shorter events, 146.9 us)
Async XLA Ops:
  154.8 22.2 %all-to-all-start.1 = ((f32[64,1,512]{2,1,0:T(1,128)}), f32[64,1,512]{2,1,0:T(1,128)S(1)}, u32[]{:S(2)}, u32[]{:S(2)}) async-start(f32[64,1,512]{2,1,0:T(1,128)} %reshape.271), calls=%async_computation.1 | async-start | bytes 262144 | tf_op jit(solution)/shard_map/all_to_all | solution.py:82
  177.0 15.3 %all-to-all-start = ((f32[64,1,512]{2,1,0:T(1,128)}), f32[64,1,512]{2,1,0:T(1,128)S(1)}, u32[]{:S(2)}, u32[]{:S(2)}) async-start(f32[64,1,512]{2,1,0:T(1,128)} %reshape.273), calls=%async_computation | async-start | bytes 262144 | tf_op jit(solution)/shard_map/all_to_all | solution.py:81
  182.6 137.4 %reduce-scatter.3.cloned.1.call-start = ((), (), s32[]{:S(2)}) async-start(), calls=%async_computation.4 | async-start | bytes 1310720 | tf_op jit(solution)/shard_map/reduce_scatter | solution.py:104
  276.2 200.5 %reduce-scatter.5.cloned.1.call-start = ((), (), s32[]{:S(2)}) async-start(), calls=%async_computation.5 | async-start | bytes 1310720 | tf_op jit(solution)/shard_map/reduce_scatter | solution.py:157
  320.0 67.6 %copy-start.1 = (f32[512,128]{0,1:T(8,128)S(1)}, f32[512,128]{0,1:T(8,128)}, u32[]{:S(2)}) copy-start(f32[512,128]{0,1:T(8,128)} %reduce-scatter.3.cloned.1.call-done) | copy-start | bytes 786436
  320.0 7.4 %collective-permute-start = (f32[512,128]{0,1:T(8,128)}, f32[512,128]{0,1:T(8,128)S(1)}, u32[]{:S(2)}, u32[]{:S(2)}) collective-permute-start(f32[512,128]{0,1:T(8,128)} %reduce-scatter.3.cloned.1.call-done), channel_id=1, source_target_pairs={{0,1},{1,0},{2,3},{3,2},{4,5},{5,4},{6,7},{7,6},{8,9},{9,8},{10,11... | collective-permute-start | bytes 786440 | tf_op jit(solution)/shard_map/ppermute | solution.py:18
  327.4 7.7 %collective-permute-start.1 = (f32[512,128]{0,1:T(8,128)S(1)}, f32[512,128]{0,1:T(8,128)S(1)}, u32[]{:S(2)}, u32[]{:S(2)}) collective-permute-start(f32[512,128]{0,1:T(8,128)S(1)} %collective-permute-done), channel_id=1, source_target_pairs={{0,2},{2,0},{1,3},{3,1},{4,6},{6,4},{5,7},{7,5},{8,10},{10,8},{9,1... | collective-permute-start | bytes 786440 | tf_op jit(solution)/shard_map/ppermute | solution.py:18
  335.1 5.2 %collective-permute-start.2 = (f32[512,128]{0,1:T(8,128)S(1)}, f32[512,128]{0,1:T(8,128)S(1)}, u32[]{:S(2)}, u32[]{:S(2)}) collective-permute-start(f32[512,128]{0,1:T(8,128)S(1)} %collective-permute-done.1), channel_id=1, source_target_pairs={{0,4},{4,0},{1,5},{5,1},{2,6},{6,2},{3,7},{7,3},{8,12},{12,8},{9,1... | collective-permute-start | bytes 786440 | tf_op jit(solution)/shard_map/ppermute | solution.py:18
  340.3 7.9 %collective-permute-start.3 = (f32[512,128]{0,1:T(8,128)S(1)}, f32[512,128]{0,1:T(8,128)S(1)}, u32[]{:S(2)}, u32[]{:S(2)}) collective-permute-start(f32[512,128]{0,1:T(8,128)S(1)} %collective-permute-done.2), channel_id=1, source_target_pairs={{0,8},{8,0},{1,9},{9,1},{2,10},{10,2},{3,11},{11,3},{4,12},{12,4},... | collective-permute-start | bytes 786440 | tf_op jit(solution)/shard_map/ppermute | solution.py:18
  348.2 5.2 %collective-permute-start.4 = (f32[512,128]{0,1:T(8,128)S(1)}, f32[512,128]{0,1:T(8,128)S(1)}, u32[]{:S(2)}, u32[]{:S(2)}) collective-permute-start(f32[512,128]{0,1:T(8,128)S(1)} %collective-permute-done.3), channel_id=1, source_target_pairs={{0,16},{16,0},{1,17},{17,1},{2,18},{18,2},{3,19},{19,3},{4,20},{20... | collective-permute-start | bytes 786440 | tf_op jit(solution)/shard_map/ppermute | solution.py:18
  353.4 8.9 %collective-permute-start.5 = (f32[512,128]{0,1:T(8,128)S(1)}, f32[512,128]{0,1:T(8,128)S(1)}, u32[]{:S(2)}, u32[]{:S(2)}) collective-permute-start(f32[512,128]{0,1:T(8,128)S(1)} %collective-permute-done.4), channel_id=1, source_target_pairs={{0,32},{32,0},{1,33},{33,1},{2,34},{34,2},{3,35},{35,3},{4,36},{36... | collective-permute-start | bytes 786440 | tf_op jit(solution)/shard_map/ppermute | solution.py:18
  363.5 7.9 %collective-permute-start.6 = (f32[512,128]{0,1:T(8,128)S(1)}, f32[512,128]{0,1:T(8,128)S(1)}, u32[]{:S(2)}, u32[]{:S(2)}) collective-permute-start(f32[512,128]{0,1:T(8,128)S(1)} %bitcast.149), channel_id=1, source_target_pairs={{0,64},{64,0},{128,192},{192,128},{1,65},{65,1},{129,193},{193,129... | collective-permute-start | bytes 786440 | tf_op jit(solution)/shard_map/ppermute | solution.py:18
  371.4 15.7 %collective-permute-start.7 = (f32[512,128]{0,1:T(8,128)S(1)}, f32[512,128]{0,1:T(8,128)S(1)}, u32[]{:S(2)}, u32[]{:S(2)}) collective-permute-start(f32[512,128]{0,1:T(8,128)S(1)} %collective-permute-done.6), channel_id=1, source_target_pairs={{0,128},{128,0},{64,192},{192,64},{1,129},{129,1},{65,193},{193,65... | collective-permute-start | bytes 786440 | tf_op jit(solution)/shard_map/ppermute | solution.py:18
  430.3 1.0 copy-start
Sparse Core Ops, SparseCore 0:
  276.3 43.6 reduce-scatter.2
  431.4 45.1 reduce-scatter.4
where the time goes:
time: 487 us; the launch traced here: 485 us
  waiting for transfers between devices  145 us (30%)
  other arithmetic  122 us (25%)
  local copies, waits for them, and re-layouts  97.3 us (20%)
  matrix products  38.6 us (8%)
  loops' own time  35 us (7%)
  starting transfers between devices  33.9 us (7%)
  between operations  13.7 us (3%)
    cos x32, other arithmetic, twiddle(): return (jnp.cos(angles), jnp.sin(angles))  99.5 us
    ppermute x8, waiting for transfers between devices, partner_2(): return lax.ppermute(block, axis, route)  48.7 us
    reduce_scatter x1, waiting for transfers between devices, on_device(): lax.psum_scatter(lax.map(inverse_block_term, offsets).reshape(group_rows...  45.4 us
    reduce_scatter x1, waiting for transfers between devices, on_device(): lax.psum_scatter(lax.map(forward_block_term, offsets).reshape(group_rows...  43.8 us
    dynamic_update_slice x32, local copies, waits for them, and re-layouts, on_device(): lax.map(forward_block_term, offsets)  34.1 us
    another operation x1, loops' own time, on_device(): lax.map(row_block, jnp.arange(block_count, dtype=jnp.int32) * block_width)  33.6 us
    dot_general x16, matrix products, row_block(): jnp.dot(stacked, tables, precision=exact_mode, preferred_element_type=jnp...  19.2 us
    unnamed x11, local copies, waits for them, and re-layouts  18.1 us
  transfers between devices with their start and end apart: 12, of which 12 were waited for; matrix products, arithmetic and copies ran while one was open for 3% of the time, Pallas kernels for 0%

commit v1 on v0

v1 whole, which is shorter than its diff:
```python
import functools
import math

import jax
import jax.numpy as jnp
import numpy as np
from jax import lax
from jax.experimental import pallas as pl
from jax.experimental.pallas import tpu as pltpu
from jax.sharding import PartitionSpec as P

MESH = pl.DeviceIdType.MESH
BLOCK = 128
WAVES = 256
PER_SLAB = 32

def fit(values, degree):
    nodes = 0.125 + 0.125 * np.cos(np.pi * (np.arange(64) + 0.5) / 64)
    series = np.polynomial.Polynomial.fit(nodes, values(np.sqrt(nodes)), degree, domain=[0, 0.25])
    return [float(c) for c in series.convert().coef]


SIN_TERMS = fit(lambda t: np.sin(np.pi * t) / t, 5)
COS_TERMS = fit(lambda t: np.cos(np.pi * t), 5)


def horner(terms, square):
    total = terms[-1]
    for term in terms[-2::-1]:
        total = total * square + term
    return total


def turn(cycles):
    t = cycles - jnp.floor(cycles + 0.5)
    square = t * t
    sine = t * horner(SIN_TERMS, square)
    cosine = horner(COS_TERMS, square)
    return 1.0 - 2.0 * sine * sine, 2.0 * sine * cosine


def split(values):
    high = values.astype(jnp.bfloat16)
    return high, (values - high.astype(jnp.float32)).astype(jnp.bfloat16)


def kernel(
    sizes,
    u_ref,
    v_ref,
    ky_ref,
    filter_hbm,
    out_ref,
    rows_ref,
    sent,
    near,
    far,
    near_side,
    far_side,
    side_out,
    side_in,
    filters,
    sem,
):
    length_y, pens, depth = sizes
    grp, pen = lax.axis_index("grp"), lax.axis_index("pen")
    core = grp % 2
    other = (grp + 2) % 4
    sibling = grp + 1 - 2 * core
    slabs = WAVES // PER_SLAB
    blocks = length_y // BLOCK
    chunks = length_y // WAVES

    barrier = pltpu.get_barrier_semaphore()

    def greet(step, carry):
        target = (pen + step) % pens
        pl.semaphore_signal(barrier, 1, device_id=(other, target), device_id_type=MESH)

        @pl.when(step > 0)
        def _():
            pl.semaphore_signal(barrier, 1, device_id=(grp, target), device_id_type=MESH)

        return carry

    lax.fori_loop(0, pens, greet, 0)
    pl.semaphore_signal(barrier, 1, device_id=(sibling, pen), device_id_type=MESH)

    load = pltpu.make_async_copy(filter_hbm, filters, sem.at[0])
    load.start()

    for b in range(blocks):
        cells = slice(b * BLOCK, (b + 1) * BLOCK)
        piece = jnp.concatenate(
            [u_ref[0, :, cells], u_ref[1, :, cells], v_ref[0, :, cells], v_ref[1, :, cells]], 0
        )
        high, low = split(piece)
        rows_ref[b * 32 : (b + 1) * 32, :] = jnp.concatenate([high, low, high], 1)

    norm = 1.0 / math.sqrt(length_y)
    lane = lax.broadcasted_iota(jnp.int32, (8, 128), 1) // PER_SLAB

    def transform(step):
        chunk = (pen // slabs + step) % chunks
        first = pl.multiple_of(chunk * WAVES, WAVES)
        waves = ky_ref[:, pl.ds(first, WAVES)].astype(jnp.float32)
        cell = lax.broadcasted_iota(jnp.int32, (BLOCK, WAVES), 0).astype(jnp.float32)
        cosine, sine = turn(cell * waves * (1.0 / length_y))
        high, low = split(jnp.concatenate([cosine, sine], 1))
        table = jnp.concatenate([high, high, low], 0)
        product = jnp.dot(rows_ref[...], table, preferred_element_type=jnp.float32)
        start = lax.broadcasted_iota(jnp.int32, (blocks, WAVES), 0).astype(jnp.float32)
        outer_cos, outer_sin = turn(start * waves * (BLOCK / length_y))
        real = jnp.zeros((32, WAVES), jnp.float32)
        imag = jnp.zeros((32, WAVES), jnp.float32)
        for b in range(blocks):
            part_cos = product[b * 32 : (b + 1) * 32, :WAVES]
            part_sin = product[b * 32 : (b + 1) * 32, WAVES:]
            c, s = outer_cos[b : b + 1], outer_sin[b : b + 1]
            real = real + (part_cos * c - part_sin * s)
            imag = imag + (part_cos * s + part_sin * c)
        signed = jnp.where(waves < length_y // 2, waves, waves - length_y)
        signed = jnp.where(waves == length_y // 2, 0.0, signed)
        scale = norm * 2.0 / length_y * signed
        pieces = (
            (-norm * imag[16:24], -norm * imag[24:32], -norm * real[16:24], -norm * real[24:32]),
            (scale * imag[0:8], scale * imag[8:16], scale * real[0:8], scale * real[8:16]),
        )
        for slab in range(slabs):
            half = slice(slab // 4 * 128, slab // 4 * 128 + 128)
            for field in range(2):
                merged = None
                for at in range(4):
                    value = pieces[field][at][:, half]
                    shift = (at - slab) % 4 * PER_SLAB
                    if shift:
                        value = pltpu.roll(value, shift, 1)
                    merged = value if merged is None else jnp.where(lane == at, value, merged)
                sent[chunk * slabs + slab, field * 8 : field * 8 + 8, :] = merged
        return chunk

    def near_copy(target):
        return pltpu.make_async_remote_copy(
            src_ref=sent.at[target],
            dst_ref=near.at[pen],
            send_sem=sem.at[1],
            recv_sem=sem.at[2],
            device_id=(grp, target),
            device_id_type=MESH,
        )

    def far_copy(target):
        return pltpu.make_async_remote_copy(
            src_ref=sent.at[target, pl.ds(0, 8)],
            dst_ref=far.at[pen],
            send_sem=sem.at[3],
            recv_sem=sem.at[4],
            device_id=(other, target),
            device_id_type=MESH,
        )

    def chunk_step(step, carry):
        chunk = transform(step)

        @pl.when(step == 0)
        def _():
            pl.semaphore_wait(barrier, 2 * pens)

        def send(at, inner):
            target = chunk * slabs + (pen + at) % slabs
            far_copy(target).start()

            @pl.when(target != pen)
            def _():
                near_copy(target).start()

            return inner

        return lax.fori_loop(0, slabs, send, carry)

    lax.fori_loop(0, chunks, chunk_step, 0)
    keep = pltpu.make_async_copy(sent.at[pen], near.at[pen], sem.at[5])
    keep.start()

    load.wait()
    keep.wait()
    ahead, behind = 1 + 2 * core, 3 - 2 * core

    def filtered(block, data, kept):
        high, low = split(data)
        taps = filters[block]
        size = data.shape[0]
        wide = jnp.dot(
            taps[:, :size],
            jnp.concatenate([high, low], 1),
            preferred_element_type=jnp.float32,
        )
        narrow = jnp.dot(taps[:, size:], high, preferred_element_type=jnp.float32)
        total = wide[:, :128] + wide[:, 128:] + narrow
        return total if kept is None else total + kept

    pltpu.make_async_copy(near.at[pl.ds(0, pens - 1)], near.at[pl.ds(0, pens - 1)], sem.at[2]).wait()
    own_data = near[:, 0:8, :].reshape(depth, 128)
    side_out[...] = filtered(ahead, own_data, None)
    near_side[...] = filtered(0, own_data, near[:, 8:16, :].reshape(depth, 128))
    pltpu.make_async_copy(far, far, sem.at[4]).wait()
    far_data = far[...].reshape(depth, 128)
    side_out[...] = filtered(behind, far_data, side_out[...])
    across = pltpu.make_async_remote_copy(
        src_ref=side_out,
        dst_ref=side_in,
        send_sem=sem.at[6],
        recv_sem=sem.at[7],
        device_id=(sibling, pen),
        device_id_type=MESH,
    )
    across.start()
    far_side[...] = filtered(2, far_data, near_side[...])
    across.wait()
    out_ref[...] = (far_side[...] + side_in[...]).T
    pltpu.make_async_copy(sent.at[pl.ds(0, pens - 1)], sent.at[pl.ds(0, pens - 1)], sem.at[1]).wait()
    pltpu.make_async_copy(far, far, sem.at[3]).wait()


def filter_table(length, groups):
    waves = np.arange(length)
    scale = np.where(waves < length // 2, waves, waves - length).astype(np.float64)
    scale[length // 2] = 0.0
    taps = np.fft.ifft(2.0 / length * scale).imag
    depth = length // groups
    cell = np.arange(depth)
    table = np.stack([taps[(depth * d + cell[:, None] - cell[None, :]) % length] for d in range(groups)])
    table = table.astype(np.float32)
    high = table.astype(jnp.bfloat16)
    low = (table - high.astype(np.float32)).astype(jnp.bfloat16)
    return np.concatenate([high, low], 2)


def on_device(u_field, v_field, ky_order):
    planes, entry_rows, length_y = u_field.shape
    pens = lax.axis_size("pen")
    groups = lax.axis_size("grp")
    depth = entry_rows * pens
    table = jnp.asarray(filter_table(depth * groups, groups))
    vmem = pl.BlockSpec(memory_space=pltpu.VMEM)
    result = pl.pallas_call(
        functools.partial(kernel, (length_y, pens, depth)),
        out_shape=jax.ShapeDtypeStruct((128, depth), jnp.float32),
        in_specs=[vmem, vmem, vmem, pl.BlockSpec(memory_space=pl.ANY)],
        out_specs=vmem,
        scratch_shapes=[
            pltpu.VMEM((length_y // BLOCK * 32, 3 * BLOCK), jnp.bfloat16),
            pltpu.VMEM((pens, 16, 128), jnp.float32),
            pltpu.VMEM((pens, 16, 128), jnp.float32),
            pltpu.VMEM((pens, 8, 128), jnp.float32),
            pltpu.VMEM((depth, 128), jnp.float32),
            pltpu.VMEM((depth, 128), jnp.float32),
            pltpu.VMEM((depth, 128), jnp.float32),
            pltpu.VMEM((depth, 128), jnp.float32),
            pltpu.VMEM((groups, depth, 2 * depth), jnp.bfloat16),
            pltpu.SemaphoreType.DMA((8,)),
        ],
        compiler_params=pltpu.CompilerParams(
            collective_id=0, has_side_effects=True, vmem_limit_bytes=48 * 1024 * 1024
        ),
    )(u_field, v_field, ky_order.reshape(1, length_y), table)
    result = result.reshape(2, planes, length_y // pens, depth)
    return jnp.transpose(result, (3, 0, 1, 2))


def solution(mesh):
    placed = (P(None, ("grp", "pen"), None), P(None, ("grp", "pen"), None), P())
    return jax.shard_map(
        on_device,
        mesh=mesh,
        in_specs=placed,
        out_specs=P("grp", None, None, "pen"),
        check_vma=False,
    )
```

time: 487 us -> 41.5 us (0.09)
  waiting for transfers between devices: 145 us -> 0 us
  other arithmetic: 122 us -> 0 us
  local copies, waits for them, and re-layouts: 97.3 us -> 5.4 us
  matrix products: 38.6 us -> 0 us
  Pallas kernels: 0 us -> 35.9 us
  loops' own time: 35 us -> 0 us
  starting transfers between devices: 33.9 us -> 0 us
  between operations: 13.7 us -> 0.01 us
    cos x32 -> x0, other arithmetic: 99.5 us -> none  [twiddle(): return (jnp.cos(angles), jnp.sin(angles))]
    reduce_scatter x2 -> x0, waiting for transfers between devices: 89.1 us -> none  [the longest x1 45.4 us: on_device(): lax.psum_scatter(lax.map(inverse_block_term, offsets).reshape(group_rows...]
    ppermute x8 -> x0, waiting for transfers between devices: 48.7 us -> none  [partner_2(): return lax.ppermute(block, axis, route)]
    dot_general x32 -> x0, matrix products: 38.6 us -> none  [the longest x16 19.2 us: row_block(): jnp.dot(stacked, tables, precision=exact_mode, preferred_element_type=jnp...]
    pallas_call x0 -> x1, Pallas kernels: none -> 35.9 us  [on_device(): pl.pallas_call(functools.partial(kernel, (length_y, pens, depth)), out_sh...]
    another operation x3 -> x0, loops' own time: 35 us -> none  [the longest x1 33.6 us: on_device(): lax.map(row_block, jnp.arange(block_count, dtype=jnp.int32) * block_width)]
    dynamic_update_slice x32 -> x0, local copies, waits for them, and re-layouts: 34.1 us -> none  [on_device(): lax.map(forward_block_term, offsets)]
    dynamic_slice x48 -> x0, local copies, waits for them, and re-layouts: 32.5 us -> none  [the longest x16 12.3 us: row_block(): waves_y = lax.dynamic_slice_in_dim(ky_order, first_row, block_width)]
  transfers between devices with their start and end apart: 12 -> 0, of which waited for: 12 -> 0; matrix products, arithmetic and copies ran while one was open for 3% -> 0% of each run, Pallas kernels for 0% -> 0%
where the time goes in v1:
time: 41.5 us; the launch traced here: 41.3 us
  Pallas kernels  35.9 us (87%)
  local copies, waits for them, and re-layouts  5.4 us (13%)
    pallas_call x1, Pallas kernels, on_device(): pl.pallas_call(functools.partial(kernel, (length_y, pens, depth)), out_sh...  35.9 us
    unnamed x9, local copies, waits for them, and re-layouts  5.4 us

profile of v1, /device:TPU:1, one launch (start us, length us, event | category | flops | bytes accessed | tf_op | source)
XLA Modules:
  0.0 41.3 jit_solution(11682987880770589676)
XLA Ops:
  0.0 0.0 copy-start
  0.0 2.2 %copy-done = bf16[4,512,1024]{2,1,0:T(8,128)(2,1)S(1)} copy-done((bf16[4,512,1024]{2,1,0:T(8,128)(2,1)S(1)}, bf16[4,512,1024]{2,1,0:T(8,128)(2,1)}, u32[]{:S(2)}) %copy-start) | copy-done | bytes 4194328
  2.2 0.0 copy-start.1
  2.2 0.9 %copy-done.1 = f32[2,8,2048]{2,1,0:T(8,128)S(1)} copy-done((f32[2,8,2048]{2,1,0:T(8,128)S(1)}, f32[2,8,2048]{2,1,0:T(8,128)}, u32[]{:S(2)}) %copy-start.1) | copy-done | bytes 131096
  3.1 0.0 copy-start.2
  3.1 0.9 %copy-done.2 = f32[2,8,2048]{2,1,0:T(8,128)S(1)} copy-done((f32[2,8,2048]{2,1,0:T(8,128)S(1)}, f32[2,8,2048]{2,1,0:T(8,128)}, u32[]{:S(2)}) %copy-start.2) | copy-done | bytes 131096
  4.0 0.0 copy-start.3
  4.0 0.7 %copy-done.3 = s32[2048]{0:T(1024)S(1)} copy-done((s32[2048]{0:T(1024)S(1)}, s32[2048]{0:T(1024)}, u32[]{:S(2)}) %copy-start.3) | copy-done | bytes 8216
  4.7 35.9 %shard_map.46 = f32[128,512]{1,0:T(8,128)S(1)} custom-call(f32[2,8,2048]{2,1,0:T(8,128)S(1)} %copy-done.1, f32[2,8,2048]{2,1,0:T(8,128)S(1)} %copy-done.2, s32[1,2048]{1,0:T(1,128)S(1)} %bitcast.5, bf16[4,512,1024]{2,1,0:T(8,128)(2,1)S(1)} %copy-done), custom_call_target="tpu_custom_call" | custom-call | tf_op jit(solution)/shard_map/pallas_call | solution.py:246
  40.6 0.7 %copy.6 = f32[512,2,2,32]{0,3,2,1:T(8,128)} copy(f32[512,2,2,32]{0,3,2,1:T(8,128)S(1)} %bitcast.4) | data formatting | bytes 524288
Async XLA Ops:
  0.0 2.2 %copy-start = (bf16[4,512,1024]{2,1,0:T(8,128)(2,1)S(1)}, bf16[4,512,1024]{2,1,0:T(8,128)(2,1)}, u32[]{:S(2)}) copy-start(bf16[4,512,1024]{2,1,0:T(8,128)(2,1)} %constant.2.clone.filter_hbm) | copy-start | bytes 12582916
  2.2 0.9 %copy-start.1 = (f32[2,8,2048]{2,1,0:T(8,128)S(1)}, f32[2,8,2048]{2,1,0:T(8,128)}, u32[]{:S(2)}) copy-start(f32[2,8,2048]{2,1,0:T(8,128)} %u_ref.1) | copy-start | bytes 393220
  3.1 0.9 %copy-start.2 = (f32[2,8,2048]{2,1,0:T(8,128)S(1)}, f32[2,8,2048]{2,1,0:T(8,128)}, u32[]{:S(2)}) copy-start(f32[2,8,2048]{2,1,0:T(8,128)} %v_ref.1) | copy-start | bytes 393220
  4.0 0.7 %copy-start.3 = (s32[2048]{0:T(1024)S(1)}, s32[2048]{0:T(1024)}, u32[]{:S(2)}) copy-start(s32[2048]{0:T(1024)} %param.6) | copy-start | bytes 24580

commit v2 on v1

--- a/solution.py
+++ b/solution.py
@@ -46,11 +46,14 @@
 
 def kernel(
     sizes,
+    u_hbm,
+    v_hbm,
+    ky_hbm,
+    filter_hbm,
+    out_ref,
     u_ref,
     v_ref,
     ky_ref,
-    filter_hbm,
-    out_ref,
     rows_ref,
     sent,
     near,
@@ -61,33 +64,50 @@
     side_in,
     filters,
     sem,
+    ready,
 ):
     length_y, pens, depth = sizes
     grp, pen = lax.axis_index("grp"), lax.axis_index("pen")
     core = grp % 2
     other = (grp + 2) % 4
     sibling = grp + 1 - 2 * core
+    half = grp // 2
     slabs = WAVES // PER_SLAB
     blocks = length_y // BLOCK
-    chunks = length_y // WAVES
-
+    chunks = length_y // 2 // WAVES
+    mirrored = pen >= pens // 2
+    own_slab = jnp.where(mirrored, pens - 1 - pen, pen)
+
+    inputs = [
+        pltpu.make_async_copy(ky_hbm, ky_ref, sem.at[8]),
+        pltpu.make_async_copy(u_hbm, u_ref, sem.at[9]),
+        pltpu.make_async_copy(v_hbm, v_ref, sem.at[10]),
+    ]
+    for copy in inputs:
+        copy.start()
     barrier = pltpu.get_barrier_semaphore()
 
+    signal = functools.partial(pl.semaphore_signal, inc=1, device_id_type=MESH)
+    signal(barrier, device_id=(sibling, pen))
+
     def greet(step, carry):
-        target = (pen + step) % pens
-        pl.semaphore_signal(barrier, 1, device_id=(other, target), device_id_type=MESH)
-
-        @pl.when(step > 0)
-        def _():
-            pl.semaphore_signal(barrier, 1, device_id=(grp, target), device_id_type=MESH)
-
+        signal(barrier, device_id=(grp, (pen + step) % pens))
         return carry
 
-    lax.fori_loop(0, pens, greet, 0)
-    pl.semaphore_signal(barrier, 1, device_id=(sibling, pen), device_id_type=MESH)
+    lax.fori_loop(1, pens, greet, 0)
+
+    @pl.when(half == 0)
+    def _():
+        def greet_far(step, carry):
+            signal(barrier, device_id=(other, (pen + step) % pens))
+            return carry
+
+        lax.fori_loop(0, pens, greet_far, 0)
 
     load = pltpu.make_async_copy(filter_hbm, filters, sem.at[0])
     load.start()
+    for copy in inputs:
+        copy.wait()
 
     for b in range(blocks):
         cells = slice(b * BLOCK, (b + 1) * BLOCK)
@@ -100,12 +120,17 @@
     norm = 1.0 / math.sqrt(length_y)
     lane = lax.broadcasted_iota(jnp.int32, (8, 128), 1) // PER_SLAB
 
+    def nth_chunk(step):
+        return (own_slab // slabs + step) % chunks
+
     def transform(step):
-        chunk = (pen // slabs + step) % chunks
+        chunk = nth_chunk(step)
         first = pl.multiple_of(chunk * WAVES, WAVES)
         waves = ky_ref[:, pl.ds(first, WAVES)].astype(jnp.float32)
         cell = lax.broadcasted_iota(jnp.int32, (BLOCK, WAVES), 0).astype(jnp.float32)
         cosine, sine = turn(cell * waves * (1.0 / length_y))
+        parity = 1.0 - 2.0 * (lax.broadcasted_iota(jnp.int32, (BLOCK, WAVES), 0) % 2).astype(jnp.float32)
+        sine = jnp.where(waves == 0, parity, jnp.where(waves == length_y // 2, 1.0, sine))
         high, low = split(jnp.concatenate([cosine, sine], 1))
         table = jnp.concatenate([high, high, low], 0)
         product = jnp.dot(rows_ref[...], table, preferred_element_type=jnp.float32)
@@ -137,21 +162,22 @@
                         value = pltpu.roll(value, shift, 1)
                     merged = value if merged is None else jnp.where(lane == at, value, merged)
                 sent[chunk * slabs + slab, field * 8 : field * 8 + 8, :] = merged
-        return chunk
-
-    def near_copy(target):
+        return None
+
+    def near_copy(field, slab, target):
+        part = pl.ds(field * 8, 8)
         return pltpu.make_async_remote_copy(
-            src_ref=sent.at[target],
-            dst_ref=near.at[pen],
+            src_ref=sent.at[slab, part],
+            dst_ref=near.at[pen, part],
             send_sem=sem.at[1],
-            recv_sem=sem.at[2],
+            recv_sem=sem.at[2 + 9 * field],
             device_id=(grp, target),
             device_id_type=MESH,
         )
 
-    def far_copy(target):
+    def far_copy(slab, target):
         return pltpu.make_async_remote_copy(
-            src_ref=sent.at[target, pl.ds(0, 8)],
+            src_ref=sent.at[slab, pl.ds(0, 8)],
             dst_ref=far.at[pen],
             send_sem=sem.at[3],
             recv_sem=sem.at[4],
@@ -159,28 +185,87 @@
             device_id_type=MESH,
         )
 
-    def chunk_step(step, carry):
-        chunk = transform(step)
-
-        @pl.when(step == 0)
-        def _():
-            pl.semaphore_wait(barrier, 2 * pens)
-
-        def send(at, inner):
-            target = chunk * slabs + (pen + at) % slabs
-            far_copy(target).start()
+    def nth(at):
+        place = (pen + at) % (2 * slabs)
+        slab = nth_chunk(at // (2 * slabs)) * slabs + place % slabs
+        return slab, jnp.where(place < slabs, slab, pens - 1 - slab)
+
+    def send_near(field, low, high):
+        def body(at, carry):
+            slab, target = nth(at)
 
             @pl.when(target != pen)
             def _():
-                near_copy(target).start()
-
-            return inner
-
-        return lax.fori_loop(0, slabs, send, carry)
+                near_copy(field, slab, target).start()
+
+            return carry
+
+        lax.fori_loop(low * 2 * slabs, high * 2 * slabs, body, 0)
+
+    def send_far(low, high):
+        def body(at, carry):
+            far_copy(*nth(at)).start()
+            return carry
+
+        lax.fori_loop(low * 2 * slabs, high * 2 * slabs, body, 0)
+
+    across = pen // 4 % 4 + pen % 4
+    hold = jnp.where(half == 0, (pen // 16 + across) // 2, across * 3 // 4)
+    hold = jnp.maximum(chunks - 1 - hold, 0)
+
+    def chunk_step(step, carry):
+        transform(step)
+
+        @pl.when(step == hold)
+        def _():
+            pl.semaphore_wait(barrier, jnp.where(half == 0, pens, 2 * pens))
+
+        low = jnp.where(step == hold, 0, step)
+
+        @pl.when((half == 1) & (step == hold))
+        def _():
+            def answer(at, inner):
+                signal(ready, device_id=(other, (pen + at) % pens))
+                return inner
+
+            lax.fori_loop(0, pens, answer, 0)
+
+        @pl.when((half == 1) & (step >= hold))
+        def _():
+            send_far(low, step + 1)
+
+        @pl.when(step >= hold)
+        def _():
+            send_near(0, low, step + 1)
+
+        return carry
 
     lax.fori_loop(0, chunks, chunk_step, 0)
-    keep = pltpu.make_async_copy(sent.at[pen], near.at[pen], sem.at[5])
+    keep = pltpu.make_async_copy(sent.at[own_slab], near.at[pen], sem.at[5])
     keep.start()
+    send_near(1, 0, chunks)
+
+    @pl.when(half == 0)
+    def _():
+        pl.semaphore_wait(ready, pens)
+        send_far(0, chunks)
+
+    block = ky_ref[:, pl.ds(pl.multiple_of(own_slab // 4 * 128, 128), 128)]
+    lane1 = lax.broadcasted_iota(jnp.int32, (1, 128), 1)
+    waves = jnp.zeros((1, 128), jnp.int32)
+    for at in range(4):
+        shifted = pltpu.roll(block, (at - own_slab % 4 + 4) % 4 * PER_SLAB, 1)
+        waves = jnp.where(lane1 // PER_SLAB == at, shifted, waves)
+    alone = jnp.broadcast_to((waves == 0) | (waves == length_y // 2), (128, 128))
+    row = lax.broadcasted_iota(jnp.int32, (128, 128), 0)
+    column = lax.broadcasted_iota(jnp.int32, (128, 128), 1)
+    plain = jnp.where((row == column) & ~(alone & (row < 64)), 1.0, 0.0)
+    reverse = row // PER_SLAB * PER_SLAB + PER_SLAB - 1 - row % PER_SLAB
+    turned = jnp.where((reverse == column) & ~alone, jnp.where(row < 64, 1.0, -1.0), 0.0)
+    turned = jnp.where((reverse - 64 == column) & alone, -1.0, turned)
+    pick = jnp.where(mirrored, turned, plain).astype(jnp.bfloat16)
+    pick = jnp.concatenate([pick, pick, pick], 1)
+    flip = jnp.where(mirrored, -1.0, 1.0)
 
     load.wait()
     keep.wait()
@@ -199,14 +284,18 @@
         total = wide[:, :128] + wide[:, 128:] + narrow
         return total if kept is None else total + kept
 
-    pltpu.make_async_copy(near.at[pl.ds(0, pens - 1)], near.at[pl.ds(0, pens - 1)], sem.at[2]).wait()
+    def received(at):
+        count = near.at[pl.ds(0, pens - 1), pl.ds(0, 8)]
+        pltpu.make_async_copy(count, count, sem.at[at]).wait()
+
+    received(2)
     own_data = near[:, 0:8, :].reshape(depth, 128)
     side_out[...] = filtered(ahead, own_data, None)
-    near_side[...] = filtered(0, own_data, near[:, 8:16, :].reshape(depth, 128))
+    near_side[...] = filtered(0, own_data, None)
     pltpu.make_async_copy(far, far, sem.at[4]).wait()
     far_data = far[...].reshape(depth, 128)
     side_out[...] = filtered(behind, far_data, side_out[...])
-    across = pltpu.make_async_remote_copy(
+    swap = pltpu.make_async_remote_copy(
         src_ref=side_out,
         dst_ref=side_in,
         send_sem=sem.at[6],
@@ -214,11 +303,21 @@
         device_id=(sibling, pen),
         device_id_type=MESH,
     )
-    across.start()
+    swap.start()
     far_side[...] = filtered(2, far_data, near_side[...])
-    across.wait()
-    out_ref[...] = (far_side[...] + side_in[...]).T
-    pltpu.make_async_copy(sent.at[pl.ds(0, pens - 1)], sent.at[pl.ds(0, pens - 1)], sem.at[1]).wait()
+    received(11)
+    swap.wait()
+    total = near[:, 8:16, :].reshape(depth, 128) + flip * (far_side[...] + side_in[...])
+    high, low = split(total)
+    lowest = (total - high.astype(jnp.float32) - low.astype(jnp.float32)).astype(jnp.bfloat16)
+    out_ref[...] = lax.dot_general(
+        pick,
+        jnp.concatenate([high, low, lowest], 1),
+        (((1,), (1,)), ((), ())),
+        preferred_element_type=jnp.float32,
+    )
+    both = near.at[pl.ds(0, pens - 1)]
+    pltpu.make_async_copy(both, both, sem.at[1]).wait()
     pltpu.make_async_copy(far, far, sem.at[3]).wait()
 
 
@@ -242,15 +341,20 @@
     groups = lax.axis_size("grp")
     depth = entry_rows * pens
     table = jnp.asarray(filter_table(depth * groups, groups))
+    inputs = (u_field, v_field, ky_order.reshape(1, length_y), table)
+    inputs = [pltpu.with_memory_space_constraint(value, pltpu.HBM) for value in inputs]
     vmem = pl.BlockSpec(memory_space=pltpu.VMEM)
     result = pl.pallas_call(
         functools.partial(kernel, (length_y, pens, depth)),
         out_shape=jax.ShapeDtypeStruct((128, depth), jnp.float32),
-        in_specs=[vmem, vmem, vmem, pl.BlockSpec(memory_space=pl.ANY)],
+        in_specs=[pl.BlockSpec(memory_space=pltpu.HBM)] * 4,
         out_specs=vmem,
         scratch_shapes=[
+            pltpu.VMEM(u_field.shape, jnp.float32),
+            pltpu.VMEM(v_field.shape, jnp.float32),
+            pltpu.VMEM((1, length_y), jnp.int32),
             pltpu.VMEM((length_y // BLOCK * 32, 3 * BLOCK), jnp.bfloat16),
-            pltpu.VMEM((pens, 16, 128), jnp.float32),
+            pltpu.VMEM((pens // 2, 16, 128), jnp.float32),
             pltpu.VMEM((pens, 16, 128), jnp.float32),
             pltpu.VMEM((pens, 8, 128), jnp.float32),
             pltpu.VMEM((depth, 128), jnp.float32),
@@ -258,12 +362,13 @@
             pltpu.VMEM((depth, 128), jnp.float32),
             pltpu.VMEM((depth, 128), jnp.float32),
             pltpu.VMEM((groups, depth, 2 * depth), jnp.bfloat16),
-            pltpu.SemaphoreType.DMA((8,)),
+            pltpu.SemaphoreType.DMA((12,)),
+            pltpu.SemaphoreType.REGULAR,
         ],
         compiler_params=pltpu.CompilerParams(
-            collective_id=0, has_side_effects=True, vmem_limit_bytes=48 * 1024 * 1024
+            collective_id=0, has_side_effects=True, vmem_limit_bytes=32 * 1024 * 1024
         ),
-    )(u_field, v_field, ky_order.reshape(1, length_y), table)
+    )(*inputs)
     result = result.reshape(2, planes, length_y // pens, depth)
     return jnp.transpose(result, (3, 0, 1, 2))
 

time: 41.5 us -> 33 us (0.80)
  the two profiles are of different devices: /device:TPU:1 before, /device:TPU:193 now
where the time goes in v2:
time: 33 us; the launch traced here: 32.9 us
  Pallas kernels  32.2 us (98%)
  local copies, waits for them, and re-layouts  0.71 us (2%)
    pallas_call x1, Pallas kernels, on_device(): pl.pallas_call(functools.partial(kernel, (length_y, pens, depth)), out_sh...  32.2 us
    unnamed x1, local copies, waits for them, and re-layouts  0.71 us

profile of v2, /device:TPU:193, one launch (start us, length us, event | category | flops | bytes accessed | tf_op | source)
XLA Modules:
  0.0 32.9 jit_solution(699957104165582307)
XLA Ops:
  0.0 32.2 %shard_map.46 = f32[128,512]{1,0:T(8,128)S(1)} custom-call(f32[2,8,2048]{2,1,0:T(8,128)} %u_hbm.1, f32[2,8,2048]{2,1,0:T(8,128)} %v_hbm.1, s32[1,2048]{1,0:T(1,128)} %bitcast.5, bf16[4,512,1024]{2,1,0:T(8,128)(2,1)} %constant.2.clone.filter_hbm), custom_call_target="tpu_custom_call" | custom-call | tf_op jit(solution)/shard_map/pallas_call | solution.py:347
  32.2 0.7 %copy.6 = f32[512,2,2,32]{0,3,2,1:T(8,128)} copy(f32[512,2,2,32]{0,3,2,1:T(8,128)S(1)} %bitcast.4) | data formatting | bytes 524288

commit v3 on v2

--- a/solution.py
+++ b/solution.py
@@ -77,6 +77,8 @@
     chunks = length_y // 2 // WAVES
     mirrored = pen >= pens // 2
     own_slab = jnp.where(mirrored, pens - 1 - pen, pen)
+    own_class = own_slab // slabs
+    slot = own_class * 2 * slabs + jnp.where(mirrored, slabs, 0) + own_slab % slabs
 
     inputs = [
         pltpu.make_async_copy(ky_hbm, ky_ref, sem.at[8]),
@@ -94,7 +96,7 @@
         signal(barrier, device_id=(grp, (pen + step) % pens))
         return carry
 
-    lax.fori_loop(1, pens, greet, 0)
+    lax.fori_loop(1, pens, greet, 0, unroll=7)
 
     @pl.when(half == 0)
     def _():
@@ -102,7 +104,7 @@
             signal(barrier, device_id=(other, (pen + step) % pens))
             return carry
 
-        lax.fori_loop(0, pens, greet_far, 0)
+        lax.fori_loop(0, pens, greet_far, 0, unroll=8)
 
     load = pltpu.make_async_copy(filter_hbm, filters, sem.at[0])
     load.start()
@@ -168,19 +170,19 @@
         part = pl.ds(field * 8, 8)
         return pltpu.make_async_remote_copy(
             src_ref=sent.at[slab, part],
-            dst_ref=near.at[pen, part],
+            dst_ref=near.at[pen if field else slot, part],
             send_sem=sem.at[1],
             recv_sem=sem.at[2 + 9 * field],
             device_id=(grp, target),
             device_id_type=MESH,
         )
 
-    def far_copy(slab, target):
+    def far_copy(slab, target, piece):
         return pltpu.make_async_remote_copy(
             src_ref=sent.at[slab, pl.ds(0, 8)],
-            dst_ref=far.at[pen],
+            dst_ref=far.at[slot],
             send_sem=sem.at[3],
-            recv_sem=sem.at[4],
+            recv_sem=sem.at[4 + 8 * piece],
             device_id=(other, target),
             device_id_type=MESH,
         )
@@ -204,7 +206,7 @@
 
     def send_far(low, high):
         def body(at, carry):
-            far_copy(*nth(at)).start()
+            far_copy(*nth(at), at // (4 * slabs)).start()
             return carry
 
         lax.fori_loop(low * 2 * slabs, high * 2 * slabs, body, 0)
@@ -224,11 +226,7 @@
 
         @pl.when((half == 1) & (step == hold))
         def _():
-            def answer(at, inner):
-                signal(ready, device_id=(other, (pen + at) % pens))
-                return inner
-
-            lax.fori_loop(0, pens, answer, 0)
+            signal(ready, device_id=(other, pen))
 
         @pl.when((half == 1) & (step >= hold))
         def _():
@@ -241,14 +239,21 @@
         return carry
 
     lax.fori_loop(0, chunks, chunk_step, 0)
-    keep = pltpu.make_async_copy(sent.at[own_slab], near.at[pen], sem.at[5])
-    keep.start()
-    send_near(1, 0, chunks)
+    keep_v = pltpu.make_async_copy(
+        sent.at[own_slab, pl.ds(0, 8)], near.at[slot, pl.ds(0, 8)], sem.at[5]
+    )
+    keep_u = pltpu.make_async_copy(
+        sent.at[own_slab, pl.ds(8, 8)], near.at[pen, pl.ds(8, 8)], sem.at[13]
+    )
+    keep_v.start()
+    keep_u.start()
 
     @pl.when(half == 0)
     def _():
-        pl.semaphore_wait(ready, pens)
+        pl.semaphore_wait(ready, 1)
         send_far(0, chunks)
+
+    send_near(1, 0, chunks)
 
     block = ky_ref[:, pl.ds(pl.multiple_of(own_slab // 4 * 128, 128), 128)]
     lane1 = lax.broadcasted_iota(jnp.int32, (1, 128), 1)
@@ -268,7 +273,8 @@
     flip = jnp.where(mirrored, -1.0, 1.0)
 
     load.wait()
-    keep.wait()
+    keep_v.wait()
+    keep_u.wait()
     ahead, behind = 1 + 2 * core, 3 - 2 * core
 
     def filtered(block, data, kept):
@@ -292,21 +298,54 @@
     own_data = near[:, 0:8, :].reshape(depth, 128)
     side_out[...] = filtered(ahead, own_data, None)
     near_side[...] = filtered(0, own_data, None)
-    pltpu.make_async_copy(far, far, sem.at[4]).wait()
-    far_data = far[...].reshape(depth, 128)
-    side_out[...] = filtered(behind, far_data, side_out[...])
-    swap = pltpu.make_async_remote_copy(
-        src_ref=side_out,
-        dst_ref=side_in,
-        send_sem=sem.at[6],
-        recv_sem=sem.at[7],
-        device_id=(sibling, pen),
-        device_id_type=MESH,
-    )
-    swap.start()
-    far_side[...] = filtered(2, far_data, near_side[...])
+    def far_part(block, piece, rows):
+        data, high_taps, low_taps = [], [], []
+        for at in range(2):
+            sender = (own_class + 2 * chunks - 2 * piece - at) % chunks
+            cells = 2 * slabs * 8
+            first = pl.multiple_of(sender * cells, cells)
+            data.append(far[pl.ds(sender * 2 * slabs, 2 * slabs)].reshape(cells, 128))
+            high_taps.append(filters[block, rows, pl.ds(first, cells)])
+            low_taps.append(filters[block, rows, pl.ds(first + depth, cells)])
+        high, low = split(jnp.concatenate(data, 0))
+        wide = jnp.dot(
+            jnp.concatenate(high_taps, 1),
+            jnp.concatenate([high, low], 1),
+            preferred_element_type=jnp.float32,
+        )
+        narrow = jnp.dot(
+            jnp.concatenate(low_taps, 1), high, preferred_element_type=jnp.float32
+        )
+        return wide[:, :128] + wide[:, 128:] + narrow
+
+    def far_received(piece):
+        count = far.at[pl.ds(0, pens // 2)]
+        pltpu.make_async_copy(count, count, sem.at[4 + 8 * piece]).wait()
+
+    every = pl.ds(0, depth)
+    far_received(0)
+    side_out[...] += far_part(behind, 0, every)
+    near_side[...] += far_part(2, 0, every)
+    far_received(1)
+    swaps = []
+    for at in range(2):
+        rows = pl.ds(at * depth // 2, depth // 2)
+        side_out[rows, :] += far_part(behind, 1, rows)
+        swaps.append(
+            pltpu.make_async_remote_copy(
+                src_ref=side_out.at[rows],
+                dst_ref=side_in.at[rows],
+                send_sem=sem.at[6 + 8 * at],
+                recv_sem=sem.at[7 + 8 * at],
+                device_id=(sibling, pen),
+                device_id_type=MESH,
+            )
+        )
+        swaps[at].start()
+    far_side[...] = near_side[...] + far_part(2, 1, every)
     received(11)
-    swap.wait()
+    for swap in swaps:
+        swap.wait()
     total = near[:, 8:16, :].reshape(depth, 128) + flip * (far_side[...] + side_in[...])
     high, low = split(total)
     lowest = (total - high.astype(jnp.float32) - low.astype(jnp.float32)).astype(jnp.bfloat16)
@@ -328,7 +367,11 @@
     taps = np.fft.ifft(2.0 / length * scale).imag
     depth = length // groups
     cell = np.arange(depth)
-    table = np.stack([taps[(depth * d + cell[:, None] - cell[None, :]) % length] for d in range(groups)])
+    pens = depth // 8
+    lower = np.arange(pens // 2).reshape(-1, WAVES // PER_SLAB)
+    pen = np.concatenate([lower, pens - 1 - lower], 1).reshape(-1, 1)
+    source = (pen * 8 + np.arange(8)).reshape(-1)
+    table = np.stack([taps[(depth * d + cell[:, None] - source[None, :]) % length] for d in range(groups)])
     table = table.astype(np.float32)
     high = table.astype(jnp.bfloat16)
     low = (table - high.astype(np.float32)).astype(jnp.bfloat16)
@@ -362,7 +405,7 @@
             pltpu.VMEM((depth, 128), jnp.float32),
             pltpu.VMEM((depth, 128), jnp.float32),
             pltpu.VMEM((groups, depth, 2 * depth), jnp.bfloat16),
-            pltpu.SemaphoreType.DMA((12,)),
+            pltpu.SemaphoreType.DMA((16,)),
             pltpu.SemaphoreType.REGULAR,
         ],
         compiler_params=pltpu.CompilerParams(

time: 33 us -> 30.5 us (0.924)
  the two profiles are of different devices: /device:TPU:193 before, /device:TPU:33 now
where the time goes in v3:
time: 30.5 us; the launch traced here: 30.4 us
  Pallas kernels  29.7 us (97%)
  local copies, waits for them, and re-layouts  0.71 us (2%)
    pallas_call x1, Pallas kernels, on_device(): pl.pallas_call(functools.partial(kernel, (length_y, pens, depth)), out_sh...  29.7 us
    unnamed x1, local copies, waits for them, and re-layouts  0.71 us

profile of v3, /device:TPU:33, one launch (start us, length us, event | category | flops | bytes accessed | tf_op | source)
XLA Modules:
  0.0 30.4 jit_solution(2588906616758346162)
XLA Ops:
  0.0 29.7 %shard_map.46 = f32[128,512]{1,0:T(8,128)S(1)} custom-call(f32[2,8,2048]{2,1,0:T(8,128)} %u_hbm.1, f32[2,8,2048]{2,1,0:T(8,128)} %v_hbm.1, s32[1,2048]{1,0:T(1,128)} %bitcast.5, bf16[4,512,1024]{2,1,0:T(8,128)(2,1)} %constant.2.clone.filter_hbm), custom_call_target="tpu_custom_call" | custom-call | tf_op jit(solution)/shard_map/pallas_call | solution.py:390
  29.7 0.7 %copy.6 = f32[512,2,2,32]{0,3,2,1:T(8,128)} copy(f32[512,2,2,32]{0,3,2,1:T(8,128)S(1)} %bitcast.4) | data formatting | bytes 524288

commit v4 on v3

--- a/solution.py
+++ b/solution.py
@@ -212,7 +212,7 @@
         lax.fori_loop(low * 2 * slabs, high * 2 * slabs, body, 0)
 
     across = pen // 4 % 4 + pen % 4
-    hold = jnp.where(half == 0, (pen // 16 + across) // 2, across * 3 // 4)
+    hold = jnp.where(half == 0, (pen // 16 + across) // 2, across * 2 // 3)
     hold = jnp.maximum(chunks - 1 - hold, 0)
 
     def chunk_step(step, carry):
@@ -232,7 +232,7 @@
         def _():
             send_far(low, step + 1)
 
-        @pl.when(step >= hold)
+        @pl.when((half == 0) & (step >= hold))
         def _():
             send_near(0, low, step + 1)
 
@@ -252,6 +252,10 @@
     def _():
         pl.semaphore_wait(ready, 1)
         send_far(0, chunks)
+
+    @pl.when(half == 1)
+    def _():
+        send_near(0, 0, chunks)
 
     send_near(1, 0, chunks)
 

time: 30.5 us -> 30 us (0.984)
  the two profiles are of different devices: /device:TPU:33 before, /device:TPU:1 now
where the time goes in v4:
time: 30 us; the launch traced here: 29.9 us
  Pallas kernels  29.2 us (97%)
  local copies, waits for them, and re-layouts  0.71 us (2%)
    pallas_call x1, Pallas kernels, on_device(): pl.pallas_call(functools.partial(kernel, (length_y, pens, depth)), out_sh...  29.2 us
    unnamed x1, local copies, waits for them, and re-layouts  0.71 us

profile of v4, /device:TPU:1, one launch (start us, length us, event | category | flops | bytes accessed | tf_op | source)
XLA Modules:
  0.0 29.9 jit_solution(14381603715938974114)
XLA Ops:
  0.0 29.2 %shard_map.46 = f32[128,512]{1,0:T(8,128)S(1)} custom-call(f32[2,8,2048]{2,1,0:T(8,128)} %u_hbm.1, f32[2,8,2048]{2,1,0:T(8,128)} %v_hbm.1, s32[1,2048]{1,0:T(1,128)} %bitcast.5, bf16[4,512,1024]{2,1,0:T(8,128)(2,1)} %constant.2.clone.filter_hbm), custom_call_target="tpu_custom_call" | custom-call | tf_op jit(solution)/shard_map/pallas_call | solution.py:394
  29.2 0.7 %copy.6 = f32[512,2,2,32]{0,3,2,1:T(8,128)} copy(f32[512,2,2,32]{0,3,2,1:T(8,128)S(1)} %bitcast.4) | data formatting | bytes 524288

commit v5 on v4

--- a/solution.py
+++ b/solution.py
@@ -202,14 +202,14 @@
 
             return carry
 
-        lax.fori_loop(low * 2 * slabs, high * 2 * slabs, body, 0)
+        lax.fori_loop(low * 2 * slabs, high * 2 * slabs, body, 0, unroll=4 if high is chunks else 1)
 
     def send_far(low, high):
         def body(at, carry):
             far_copy(*nth(at), at // (4 * slabs)).start()
             return carry
 
-        lax.fori_loop(low * 2 * slabs, high * 2 * slabs, body, 0)
+        lax.fori_loop(low * 2 * slabs, high * 2 * slabs, body, 0, unroll=4 if high is chunks else 1)
 
     across = pen // 4 % 4 + pen % 4
     hold = jnp.where(half == 0, (pen // 16 + across) // 2, across * 2 // 3)

time: 30 us -> 30 us (level)
  no operation moved by 1% of the time
where the time goes in v5:
time: 30 us; the launch traced here: 29.9 us
  Pallas kernels  29.2 us (97%)
  local copies, waits for them, and re-layouts  0.71 us (2%)
    pallas_call x1, Pallas kernels, on_device(): pl.pallas_call(functools.partial(kernel, (length_y, pens, depth)), out_sh...  29.2 us
    unnamed x1, local copies, waits for them, and re-layouts  0.71 us

profile of v5, /device:TPU:1, one launch (start us, length us, event | category | flops | bytes accessed | tf_op | source)
XLA Modules:
  0.0 29.9 jit_solution(12201262630569286795)
XLA Ops:
  0.0 29.2 %shard_map.46 = f32[128,512]{1,0:T(8,128)S(1)} custom-call(f32[2,8,2048]{2,1,0:T(8,128)} %u_hbm.1, f32[2,8,2048]{2,1,0:T(8,128)} %v_hbm.1, s32[1,2048]{1,0:T(1,128)} %bitcast.5, bf16[4,512,1024]{2,1,0:T(8,128)(2,1)} %constant.2.clone.filter_hbm), custom_call_target="tpu_custom_call" | custom-call | tf_op jit(solution)/shard_map/pallas_call | solution.py:394
  29.2 0.7 %copy.6 = f32[512,2,2,32]{0,3,2,1:T(8,128)} copy(f32[512,2,2,32]{0,3,2,1:T(8,128)S(1)} %bitcast.4) | data formatting | bytes 524288
